TPU v7x, 32 devices: a whole 2x2x4 slice. The times are simulated.
32 devices in a mesh: var: 4 (over y, x), lat: 4 (over z), dp: 2 (over core).
Axes of the slice: x: 2, y: 2, z: 4, core: 2. Of those that a mesh axis runs over, the one named last changes fastest.
Arguments:
- patches: bfloat16 [8, 24, 3840], P(('dp', 'var'), 'lat'), parts along dimension 0, may hold values from -6 to 6
- level_bias: bfloat16 [4, 512], replicated, may hold values from -6 to 6
- embed_weight: bfloat16 [80, 512], replicated, may hold values from -0.625 to 0.625
- latent_query: bfloat16 [3, 512], replicated, may hold values from -60 to 60
- cross_key: bfloat16 [512, 512], replicated, may hold values from -0.25 to 0.25
- cross_value: bfloat16 [512, 512], replicated, may hold values from -0.25 to 0.25
- cross_output: bfloat16 [512, 512], replicated, may hold values from -0.25 to 0.25
- first_gain: float32 [512], replicated, may hold values from 0.1 to 1.9
- window_query: bfloat16 [512, 512], replicated, may hold values from -2 to 2
- window_context: bfloat16 [512, 1024], replicated, may hold values from -0.25 to 0.25
- window_output: bfloat16 [512, 512], replicated, may hold values from -0.25 to 0.25
- second_gain: float32 [512], replicated, may hold values from 0.1 to 1.9
- up_weight: bfloat16 [512, 2048], replicated, may hold values from -0.25 to 0.25
- down_weight: bfloat16 [2048, 512], replicated, may hold values from -0.125 to 0.125
Outputs:
- encoded: bfloat16 [6, 24, 48, 512], P('dp', 'lat', 'var'), parts along dimension 0
There are 2 independent parts, one for each index of `dp`. A program takes and returns all parts, laid end to end along the dimension named above; an argument that names none is the same for every part. Nothing has to cross between parts.
All inputs are finite; a program needn't handle non-finite values.
Results may differ from a plain program's by a relative error of at most 0.013.
Values may be sent and summed in bfloat16 or wider, within the bound.
A program may use at most 64 MiB of HBM per device.

v0:
```python
import functools
import math

import jax
import jax.numpy as jnp
from jax import lax
from jax.experimental import pallas as pl
from jax.experimental.pallas import tpu as pltpu
from jax.sharding import PartitionSpec as P

HEADS = 16
WLAT = 6
WLON = 12
SHIFT = 3
LANES = 128
SUBLANES = 8

epsilon = 1e-05
masked_score = -1e30
MESH = pl.DeviceIdType.MESH
f32 = jnp.float32
bf16 = jnp.bfloat16


def round_up(value, unit):
    return -(-value // unit) * unit


def layer_norm(tensor, scales):
    center = jnp.mean(tensor, axis=-1, keepdims=True)
    offset = tensor - center
    spread = jnp.mean(offset * offset, axis=-1, keepdims=True)
    return offset * lax.rsqrt(spread + epsilon) * scales


def dot(a, b):
    return jnp.dot(a, b, preferred_element_type=f32)


def dot_nt(a, b):
    return lax.dot_general(a, b, (((1,), (1,)), ((), ())), preferred_element_type=f32)


def kernel(
    sizes,
    patches_hbm, bias_hbm, embed_hbm, query_hbm, ck_hbm, cv_hbm, co_hbm, gain1_hbm,
    wq_hbm, wc_hbm, wo_hbm, gain2_hbm, up_hbm, down_hbm,
    res_ref,
    patches_v, gathered, rows_ref, bias_v, embed_v, query_v, ck_v, cv_v, co_v, gain1_v,
    wq_v, wc_v, wo_v, gain2_v, up_v, down_v,
    straight_ref, widen_ref, token_ref, value_ref, key_ref, val_ref, ask_ref, base_ref, mix_ref,
    load_sem, send_sem, recv_sem,
):
    var_count, lat_count, level_here, rows, cols, pixels, width, channels, latents = sizes
    levels = var_count * level_here
    head = channels // HEADS
    me = lax.axis_index("var")
    band = lax.axis_index("lat")
    has_low = band > 0
    has_high = band < lat_count - 1

    barrier = pltpu.get_barrier_semaphore()

    def signal(var, lat):
        pl.semaphore_signal(
            barrier, inc=1, device_id={"var": var, "lat": lat}, device_id_type=MESH
        )

    for d in range(1, var_count):
        signal(lax.rem(me + d, var_count), band)

    @pl.when(has_low)
    def _():
        for d in range(var_count):
            signal(lax.rem(me + d, var_count), band - 1)

    @pl.when(has_high)
    def _():
        for d in range(var_count):
            signal(lax.rem(me + d, var_count), band + 1)

    pairs = (
        (query_hbm, query_v), (ck_hbm, ck_v), (embed_hbm, embed_v), (bias_hbm, bias_v),
        (cv_hbm, cv_v), (co_hbm, co_v), (gain1_hbm, gain1_v), (wc_hbm, wc_v), (wq_hbm, wq_v),
        (wo_hbm, wo_v), (gain2_hbm, gain2_v), (up_hbm, up_v), (down_hbm, down_v),
    )
    loads = [
        pltpu.make_async_copy(src, dst, load_sem.at[i]) for i, (src, dst) in enumerate(pairs)
    ]
    (l_query, l_ck, l_embed, l_bias, l_cv, l_co, l_gain1, l_wc, l_wq, l_wo, l_gain2, l_up, l_down) = loads

    def start_of(var):
        return pl.multiple_of(var * (cols * pixels) // LANES * LANES, LANES)

    own = pltpu.make_async_copy(
        patches_hbm.at[:, :, pl.ds(start_of(me), width)], gathered.at[1, me], load_sem.at[len(pairs)]
    )
    own.start()
    stage = pltpu.make_async_copy(patches_hbm, patches_v, load_sem.at[len(pairs) + 1])
    stage.start()
    for load in loads[:5]:
        load.start()

    l_query.wait()
    l_ck.wait()
    lane_head = lax.broadcasted_iota(jnp.int32, (HEADS, channels), 1) // head
    own_head = lane_head == lax.broadcasted_iota(jnp.int32, (HEADS, channels), 0)
    queries = query_v[...].astype(f32)
    spread = [jnp.where(own_head, queries[q : q + 1], 0.0) for q in range(latents)]
    spread.append(jnp.zeros((LANES - latents * HEADS, channels), f32))
    folded = dot_nt(jnp.concatenate(spread, axis=0).astype(bf16), ck_v[...]) * (
        head ** (-0.5) * math.log2(math.e)
    )
    folded_high = folded.astype(bf16)
    folded_low = (folded - folded_high.astype(f32)).astype(bf16)
    tall = rows + 2 * SHIFT
    l_embed.wait()
    l_bias.wait()
    biases = bias_v[...].astype(f32)
    row_id = lax.broadcasted_iota(jnp.int32, (LANES - pixels, channels), 0)
    level_rows = jnp.zeros((LANES - pixels, channels), f32)
    for l in range(levels):
        level_rows = jnp.where(row_id == l, biases[l : l + 1], level_rows)
    base = jnp.concatenate([embed_v[...].astype(f32), level_rows], axis=0).astype(bf16)
    l_cv.wait()
    straight = jnp.concatenate(
        [dot(base, cv_v[...]), dot_nt(base, folded_high) + dot_nt(base, folded_low)], axis=1
    )
    straight_high = straight.astype(bf16)
    straight_ref[:LANES] = straight_high
    straight_ref[LANES:] = (straight - straight_high.astype(f32)).astype(bf16)
    row_id = lax.broadcasted_iota(jnp.int32, (levels * rows, LANES), 0)
    lane_id = lax.broadcasted_iota(jnp.int32, (levels * rows, LANES), 1)
    marks = jnp.zeros((levels * rows, LANES), f32)
    for l in range(levels):
        inside = jnp.logical_and(row_id >= l * rows, row_id < (l + 1) * rows)
        marks = jnp.where(jnp.logical_and(inside, lane_id == pixels + l), 1.0, marks)
    slot = lax.rem(lax.broadcasted_iota(jnp.int32, (2 * LANES, channels), 0), LANES)
    lane = lax.broadcasted_iota(jnp.int32, (2 * LANES, channels), 1) // head
    for q in range(latents):
        widen_ref[q] = jnp.where(slot == lane + q * HEADS, 1.0, 0.0).astype(bf16)

    pl.semaphore_wait(
        barrier,
        var_count - 1 + var_count * (has_low.astype(jnp.int32) + has_high.astype(jnp.int32)),
    )

    stage.wait()

    def send(d, step):
        target = lax.rem(me + d, var_count)
        return pltpu.make_async_remote_copy(
            src_ref=patches_v.at[:, :, pl.ds(start_of(target), width)],
            dst_ref=gathered.at[1 - step, me],
            send_sem=send_sem.at[1 - step, d],
            recv_sem=recv_sem.at[1 - step, me],
            device_id={"var": target, "lat": band + step},
            device_id_type=MESH,
        )

    def arrival(d, slot):
        source = lax.rem(me + d, var_count)
        return pltpu.make_async_remote_copy(
            src_ref=patches_v.at[:, :, pl.ds(start_of(me), width)],
            dst_ref=gathered.at[slot, source],
            send_sem=send_sem.at[slot, d],
            recv_sem=recv_sem.at[slot, source],
            device_id={"var": source, "lat": band},
            device_id_type=MESH,
        )

    for d in range(1, var_count):
        send(d, 0).start()
    @pl.when(has_low)
    def _():
        for d in range(var_count):
            send(d, -1).start()

    @pl.when(has_high)
    def _():
        for d in range(var_count):
            send(d, 1).start()

    for load in loads[5:]:
        load.start()

    @pl.when(jnp.logical_not(has_low))
    def _():
        gathered[0] = jnp.zeros(gathered.shape[1:], bf16)

    @pl.when(jnp.logical_not(has_high))
    def _():
        gathered[2] = jnp.zeros(gathered.shape[1:], bf16)

    own.wait()
    used = latents * SHIFT * cols
    for w in range(2):
        if used < base_ref.shape[0] // 2:
            fill = (base_ref.shape[0] // 2) * w + used
            ask_ref[fill : (base_ref.shape[0] // 2) * (w + 1)] = jnp.zeros((base_ref.shape[0] // 2 - used, channels), f32)
            base_ref[fill : (base_ref.shape[0] // 2) * (w + 1)] = jnp.zeros((base_ref.shape[0] // 2 - used, channels), f32)
    for d in range(1, var_count):
        arrival(d, 1).wait_recv()
    l_co.wait()
    l_gain1.wait()
    grid = tall * cols
    block = rows * cols
    edge = SHIFT * cols

    def pool():
        pixel_rows = rows_ref[...]
        for phase in sorted({v * cols * pixels % LANES for v in range(var_count)}):
            if phase:
                pixel_rows = jnp.where(
                    lax.rem(me * (cols * pixels), LANES) == phase,
                    pltpu.roll(rows_ref[...], width - phase, 1),
                    pixel_rows,
                )
        for j in range(cols):
            piece = pixel_rows[:, j * pixels : j * pixels + LANES]
            token_ref[pl.ds(j, levels * rows, stride=cols), :] = jnp.where(
                lane_id < pixels, piece, marks
            )
        tokens = token_ref[...].astype(bf16)
        made = dot(jnp.concatenate([tokens, tokens], axis=1), straight_ref[...])
        value_ref[...] = made[:, :channels]
        scores = made[:, channels:]
        pieces = [scores[l * block : (l + 1) * block] for l in range(levels)]
        highest = functools.reduce(jnp.maximum, pieces)
        weights = [jnp.exp2(piece - highest) for piece in pieces]
        inverse = 1.0 / functools.reduce(jnp.add, weights)
        share = jnp.concatenate([weight * inverse for weight in weights], axis=0)
        high = share.astype(bf16)
        low = (share - high.astype(f32)).astype(bf16)
        shares = jnp.concatenate([high, low], axis=1)
        found = []
        for q in range(latents):
            parts = dot(shares, widen_ref[q]) * value_ref[...]
            total = functools.reduce(
                jnp.add, [parts[l * block : (l + 1) * block] for l in range(levels)]
            )
            found.append(total)
        joined = dot(jnp.concatenate(found, axis=0).astype(bf16), co_v[...])
        return [
            (joined[q * block : (q + 1) * block] + queries[q : q + 1]).astype(bf16).astype(f32)
            for q in range(latents)
        ]

    count = round_up(latents * SHIFT * cols, SUBLANES)
    for v in range(var_count):
        for i in range(level_here):
            at = (v * level_here + i) * rows
            rows_ref[at : at + rows] = gathered[1, v, i].astype(f32)
    l_wc.wait()
    l_wq.wait()
    window = WLAT * cols
    half = SHIFT * cols
    own_latent = jnp.concatenate(pool(), axis=0)
    own_normed = layer_norm(own_latent, gain1_v[...]).astype(bf16)
    context = dot(own_normed, wc_v[...])
    asked = dot(own_normed, wq_v[...]) * (head ** (-0.5) * math.log2(math.e))
    part = half
    for q in range(latents):
        for w in range(2):
            at = q * block + w * half
            to = (w * latents + q) * window + (1 - w) * half
            key_ref[to : to + half] = context[at : at + half, :channels]
            val_ref[to : to + half] = context[at : at + half, channels:]
            to = w * count + q * half
            ask_ref[to : to + half] = asked[at : at + half]
            base_ref[to : to + half] = own_latent[at : at + half]

    @pl.when(has_low)
    def _():
        for d in range(var_count):
            arrival(d, 0).wait_recv()

    @pl.when(has_high)
    def _():
        for d in range(var_count):
            arrival(d, 2).wait_recv()

    for v in range(var_count):
        for i in range(level_here):
            at = (v * level_here + i) * rows
            rows_ref[at : at + SHIFT] = gathered[0, v, i].astype(f32)[rows - SHIFT :]
            rows_ref[at + SHIFT : at + rows] = gathered[2, v, i].astype(f32)[:SHIFT]
    outer = pool()
    edge_normed = layer_norm(jnp.concatenate(outer, axis=0), gain1_v[...])
    edge_context = dot(edge_normed.astype(bf16), wc_v[...])
    for q in range(latents):
        at = q * block
        for w in range(2):
            to = (w * latents + q) * window + w * half
            key_ref[to : to + half] = edge_context[at + w * edge : at + (w + 1) * edge, :channels]
            val_ref[to : to + half] = edge_context[at + w * edge : at + (w + 1) * edge, channels:]

    span = latents * window
    group = LANES // head
    place = lax.rem(lax.broadcasted_iota(jnp.int32, (1, span), 1), window)
    lane_of = lax.broadcasted_iota(jnp.int32, (count, LANES), 1) // head
    empty = (
        jnp.logical_and(place < half, jnp.logical_not(has_low)),
        jnp.logical_and(place >= half, jnp.logical_not(has_high)),
    )
    for w in range(2):
        offset = jnp.where(empty[w], masked_score, 0.0)
        for g in range(channels // LANES):
            lanes = slice(g * LANES, (g + 1) * LANES)
            ask = ask_ref[w * count : (w + 1) * count, lanes]
            keys = key_ref[w * span : (w + 1) * span, lanes].astype(bf16)
            vals = val_ref[w * span : (w + 1) * span, lanes].astype(bf16)
            asks = jnp.concatenate(
                [jnp.where(lane_of == h, ask, 0.0) for h in range(group)], axis=0
            ).astype(bf16)
            logits = dot_nt(asks, keys) + offset
            power = jnp.exp2(logits - jnp.max(logits, axis=-1, keepdims=True))
            amount = jnp.sum(power, axis=-1, keepdims=True)
            taken = dot(power.astype(bf16), vals) / amount
            joined = taken[:count]
            for h in range(1, group):
                joined = jnp.where(lane_of == h, taken[h * count : (h + 1) * count], joined)
            mix_ref[w * count : (w + 1) * count, lanes] = joined

    l_wo.wait()
    l_gain2.wait()
    mixed = dot(mix_ref[...].astype(bf16), wo_v[...]) + base_ref[...]
    second = layer_norm(mixed, gain2_v[...]).astype(bf16)
    l_up.wait()
    hidden = jax.nn.gelu(dot(second, up_v[...])).astype(bf16)
    l_down.wait()
    res_ref[...] = mixed + dot(hidden, down_v[...])
    for d in range(1, var_count):
        send(d, 0).wait_send()

    @pl.when(has_low)
    def _():
        for d in range(var_count):
            send(d, -1).wait_send()

    @pl.when(has_high)
    def _():
        for d in range(var_count):
            send(d, 1).wait_send()


def finish(sizes, res_ref, out_ref):
    latents, cols, part, count = sizes
    for w in range(2):
        for q in range(latents):
            for r in range(SHIFT):
                at = w * count + q * part + r * cols
                out_ref[q, w * SHIFT + r] = res_ref[at : at + cols].astype(bf16)


def solution(mesh):
    var_count, lat_count = mesh.shape["var"], mesh.shape["lat"]

    def body(*args):
        (patches, level_bias, embed_weight, latent_query, cross_key, cross_value, cross_output,
         first_gain, window_query, window_context, window_output, second_gain, up_weight,
         down_weight) = args
        level_here, rows, flat = patches.shape
        pixels, channels = embed_weight.shape
        latents = latent_query.shape[0]
        units = up_weight.shape[1]
        cols = flat // pixels // var_count
        levels = level_here * var_count
        assert rows == WLAT == 2 * SHIFT and cols == WLON
        assert pixels + levels <= LANES >= latents * HEADS
        width = round_up(cols * pixels + max(v * cols * pixels % LANES for v in range(var_count)), LANES)
        tall = rows + 2 * SHIFT
        grid = tall * cols
        span = latents * WLAT * cols
        count = round_up(latents * SHIFT * cols, SUBLANES)
        sizes = (var_count, lat_count, level_here, rows, cols, pixels, width, channels, latents)
        operands = list(args)
        operands[7] = first_gain.reshape(1, channels)
        operands[11] = second_gain.reshape(1, channels)
        operands = [pltpu.with_memory_space_constraint(x, pltpu.HBM) for x in operands]
        any_spec = pl.BlockSpec(memory_space=pl.ANY)
        weights = [pltpu.VMEM(x.shape, x.dtype) for x in operands[1:]]
        result = pl.pallas_call(
            functools.partial(kernel, sizes),
            out_shape=jax.ShapeDtypeStruct((2 * count, channels), f32),
            in_specs=[any_spec] * len(operands),
            out_specs=pl.BlockSpec(memory_space=pltpu.VMEM),
            scratch_shapes=[
                pltpu.VMEM(args[0].shape, bf16),
                pltpu.VMEM((3, var_count, level_here, rows, width), bf16),
                pltpu.VMEM((levels * rows, width), f32),
                *weights,
                pltpu.VMEM((2 * LANES, channels + LANES), bf16),
                pltpu.VMEM((latents, 2 * LANES, channels), bf16),
                pltpu.VMEM((levels * rows * cols, LANES), f32),
                pltpu.VMEM((levels * rows * cols, channels), f32),
                pltpu.VMEM((2 * span, channels), f32),
                pltpu.VMEM((2 * span, channels), f32),
                pltpu.VMEM((2 * count, channels), f32),
                pltpu.VMEM((2 * count, channels), f32),
                pltpu.VMEM((2 * count, channels), f32),
                pltpu.SemaphoreType.DMA((len(operands) + 1,)),
                pltpu.SemaphoreType.DMA((3, var_count)),
                pltpu.SemaphoreType.DMA((3, var_count)),
            ],
            compiler_params=pltpu.CompilerParams(collective_id=0, has_side_effects=True,
                                                 vmem_limit_bytes=36 * 1024 * 1024),
        )(*operands)
        return pl.pallas_call(
            functools.partial(finish, (latents, cols, SHIFT * cols, count)),
            out_shape=jax.ShapeDtypeStruct((latents, rows, cols, channels), bf16),
            in_specs=[pl.BlockSpec(memory_space=pltpu.VMEM)],
            out_specs=pl.BlockSpec(memory_space=pltpu.VMEM),
            compiler_params=pltpu.CompilerParams(vmem_limit_bytes=16 * 1024 * 1024),
        )(result)

    return jax.shard_map(
        body,
        mesh=mesh,
        in_specs=(P(("dp", "var"), "lat", None),) + (P(),) * 13,
        out_specs=P("dp", "lat", "var", None),
        check_vma=False,
    )
```

profile of v0, /device:TPU:0, one launch (start us, length us, event | category | flops | bytes accessed | tf_op | source)
XLA Modules:
  0.0 15.4 jit_solution(9220949917781838318)
XLA Ops:
  0.0 14.7 %shard_map.136.res_ref = f32[224,512]{1,0:T(8,128)S(1)} custom-call(bf16[1,6,3840]{2,1,0:T(8,128)(2,1)} %patches_hbm.1, bf16[4,512]{1,0:T(4,128)(2,1)} %bias_hbm.1, bf16[80,512]{1,0:T(8,128)(2,1)} %embed_hbm.1, bf16[3,512]{1,0:T(4,128)(2,1)} %query_hbm.1, bf16[512,512]{1,0:T(8,128)(2,1)} %ck_hbm.1, bf16[512,512]{1,0:T(8,128)(2,1)} %cv_hbm.1, ...), custom_call_target="tpu_custom_call" | custom-call | tf_op jit(solution)/shard_map/pallas_call | solution.py:383
  14.7 0.8 %shard_map.137 = bf16[3,6,12,512]{3,2,1,0:T(8,128)(2,1)} custom-call(f32[224,512]{1,0:T(8,128)S(1)} %shard_map.136.res_ref), custom_call_target="tpu_custom_call" | custom-call | tf_op jit(solution)/shard_map/pallas_call | solution.py:409
where the time goes:
time: 15.6 us; the launch traced here: 15.4 us
  Pallas kernels  15.4 us (99%)
    pallas_call x1, Pallas kernels, body(): pl.pallas_call(functools.partial(kernel, sizes), out_shape=jax.ShapeDtype...  14.7 us
    pallas_call x1, Pallas kernels, body(): pl.pallas_call(functools.partial(finish, (latents, cols, SHIFT * cols, co...  0.75 us

commit v1 on v0

--- a/solution.py
+++ b/solution.py
@@ -49,7 +49,7 @@
     patches_v, gathered, rows_ref, bias_v, embed_v, query_v, ck_v, cv_v, co_v, gain1_v,
     wq_v, wc_v, wo_v, gain2_v, up_v, down_v,
     straight_ref, widen_ref, token_ref, value_ref, key_ref, val_ref, ask_ref, base_ref, mix_ref,
-    load_sem, send_sem, recv_sem,
+    load_sem, send_sem, recv_sem, ready_sem,
 ):
     var_count, lat_count, level_here, rows, cols, pixels, width, channels, latents = sizes
     levels = var_count * level_here
@@ -59,6 +59,16 @@
     has_low = band > 0
     has_high = band < lat_count - 1
 
+    @jax.named_scope("A_signal")
+    def announce():
+        for d in range(1, var_count):
+            signal(peer(d), band)
+
+        @pl.when(has_high)
+        def _():
+            for d in range(var_count):
+                signal(peer(d), band + 1)
+
     barrier = pltpu.get_barrier_semaphore()
 
     def signal(var, lat):
@@ -66,18 +76,20 @@
             barrier, inc=1, device_id={"var": var, "lat": lat}, device_id_type=MESH
         )
 
-    for d in range(1, var_count):
-        signal(lax.rem(me + d, var_count), band)
-
-    @pl.when(has_low)
-    def _():
-        for d in range(var_count):
-            signal(lax.rem(me + d, var_count), band - 1)
-
-    @pl.when(has_high)
-    def _():
-        for d in range(var_count):
-            signal(lax.rem(me + d, var_count), band + 1)
+    def peer(d):
+        if d == 0:
+            return me
+        if var_count & (var_count - 1):
+            return lax.rem(me + d, var_count)
+        turned = me
+        bit = 1
+        while bit < var_count:
+            if d & bit:
+                turned = turned + bit * (1 - 2 * lax.rem(me // bit, 2))
+            bit *= 2
+        return turned
+
+    announce()
 
     pairs = (
         (query_hbm, query_v), (ck_hbm, ck_v), (embed_hbm, embed_v), (bias_hbm, bias_v),
@@ -101,54 +113,17 @@
     for load in loads[:5]:
         load.start()
 
-    l_query.wait()
-    l_ck.wait()
-    lane_head = lax.broadcasted_iota(jnp.int32, (HEADS, channels), 1) // head
-    own_head = lane_head == lax.broadcasted_iota(jnp.int32, (HEADS, channels), 0)
-    queries = query_v[...].astype(f32)
-    spread = [jnp.where(own_head, queries[q : q + 1], 0.0) for q in range(latents)]
-    spread.append(jnp.zeros((LANES - latents * HEADS, channels), f32))
-    folded = dot_nt(jnp.concatenate(spread, axis=0).astype(bf16), ck_v[...]) * (
-        head ** (-0.5) * math.log2(math.e)
-    )
-    folded_high = folded.astype(bf16)
-    folded_low = (folded - folded_high.astype(f32)).astype(bf16)
-    tall = rows + 2 * SHIFT
-    l_embed.wait()
-    l_bias.wait()
-    biases = bias_v[...].astype(f32)
-    row_id = lax.broadcasted_iota(jnp.int32, (LANES - pixels, channels), 0)
-    level_rows = jnp.zeros((LANES - pixels, channels), f32)
-    for l in range(levels):
-        level_rows = jnp.where(row_id == l, biases[l : l + 1], level_rows)
-    base = jnp.concatenate([embed_v[...].astype(f32), level_rows], axis=0).astype(bf16)
-    l_cv.wait()
-    straight = jnp.concatenate(
-        [dot(base, cv_v[...]), dot_nt(base, folded_high) + dot_nt(base, folded_low)], axis=1
-    )
-    straight_high = straight.astype(bf16)
-    straight_ref[:LANES] = straight_high
-    straight_ref[LANES:] = (straight - straight_high.astype(f32)).astype(bf16)
-    row_id = lax.broadcasted_iota(jnp.int32, (levels * rows, LANES), 0)
-    lane_id = lax.broadcasted_iota(jnp.int32, (levels * rows, LANES), 1)
-    marks = jnp.zeros((levels * rows, LANES), f32)
-    for l in range(levels):
-        inside = jnp.logical_and(row_id >= l * rows, row_id < (l + 1) * rows)
-        marks = jnp.where(jnp.logical_and(inside, lane_id == pixels + l), 1.0, marks)
-    slot = lax.rem(lax.broadcasted_iota(jnp.int32, (2 * LANES, channels), 0), LANES)
-    lane = lax.broadcasted_iota(jnp.int32, (2 * LANES, channels), 1) // head
-    for q in range(latents):
-        widen_ref[q] = jnp.where(slot == lane + q * HEADS, 1.0, 0.0).astype(bf16)
-
-    pl.semaphore_wait(
-        barrier,
-        var_count - 1 + var_count * (has_low.astype(jnp.int32) + has_high.astype(jnp.int32)),
-    )
-
-    stage.wait()
+    with jax.named_scope("F_barrier"):
+        pl.semaphore_wait(
+            barrier,
+            var_count - 1 + var_count * has_low.astype(jnp.int32),
+        )
+
+    with jax.named_scope("G_stage"):
+        stage.wait()
 
     def send(d, step):
-        target = lax.rem(me + d, var_count)
+        target = peer(d)
         return pltpu.make_async_remote_copy(
             src_ref=patches_v.at[:, :, pl.ds(start_of(target), width)],
             dst_ref=gathered.at[1 - step, me],
@@ -159,7 +134,7 @@
         )
 
     def arrival(d, slot):
-        source = lax.rem(me + d, var_count)
+        source = peer(d)
         return pltpu.make_async_remote_copy(
             src_ref=patches_v.at[:, :, pl.ds(start_of(me), width)],
             dst_ref=gathered.at[slot, source],
@@ -169,40 +144,94 @@
             device_id_type=MESH,
         )
 
-    for d in range(1, var_count):
+    for d in range(var_count - 1, 0, -1):
         send(d, 0).start()
+
     @pl.when(has_low)
     def _():
         for d in range(var_count):
+            pl.semaphore_signal(
+                ready_sem, inc=1, device_id={"var": peer(d), "lat": band - 1}, device_id_type=MESH
+            )
+        for d in range(var_count - 1, -1, -1):
             send(d, -1).start()
 
-    @pl.when(has_high)
-    def _():
-        for d in range(var_count):
-            send(d, 1).start()
-
-    for load in loads[5:]:
-        load.start()
-
-    @pl.when(jnp.logical_not(has_low))
-    def _():
-        gathered[0] = jnp.zeros(gathered.shape[1:], bf16)
-
-    @pl.when(jnp.logical_not(has_high))
-    def _():
-        gathered[2] = jnp.zeros(gathered.shape[1:], bf16)
-
-    own.wait()
-    used = latents * SHIFT * cols
-    for w in range(2):
-        if used < base_ref.shape[0] // 2:
-            fill = (base_ref.shape[0] // 2) * w + used
-            ask_ref[fill : (base_ref.shape[0] // 2) * (w + 1)] = jnp.zeros((base_ref.shape[0] // 2 - used, channels), f32)
-            base_ref[fill : (base_ref.shape[0] // 2) * (w + 1)] = jnp.zeros((base_ref.shape[0] // 2 - used, channels), f32)
-    for d in range(1, var_count):
-        arrival(d, 1).wait_recv()
-    l_co.wait()
-    l_gain1.wait()
+    with jax.named_scope("H_startloads"):
+        for load in loads[5:]:
+            load.start()
+
+    with jax.named_scope("B_wait_ck"):
+        l_query.wait()
+        l_ck.wait()
+    with jax.named_scope("C_fold"):
+        lane_head = lax.broadcasted_iota(jnp.int32, (HEADS, channels), 1) // head
+        own_head = lane_head == lax.broadcasted_iota(jnp.int32, (HEADS, channels), 0)
+        queries = query_v[...].astype(f32)
+        spread = [jnp.where(own_head, queries[q : q + 1], 0.0) for q in range(latents)]
+        spread.append(jnp.zeros((LANES - latents * HEADS, channels), f32))
+        folded = dot_nt(jnp.concatenate(spread, axis=0).astype(bf16), ck_v[...]) * (
+            head ** (-0.5) * math.log2(math.e)
+        )
+        folded_high = folded.astype(bf16)
+        folded_low = (folded - folded_high.astype(f32)).astype(bf16)
+        tall = rows + 2 * SHIFT
+    with jax.named_scope("D_base"):
+        l_embed.wait()
+        l_bias.wait()
+        biases = bias_v[...].astype(f32)
+        row_id = lax.broadcasted_iota(jnp.int32, (LANES - pixels, channels), 0)
+        level_rows = jnp.zeros((LANES - pixels, channels), f32)
+        for l in range(levels):
+            level_rows = jnp.where(row_id == l, biases[l : l + 1], level_rows)
+        base = jnp.concatenate([embed_v[...].astype(f32), level_rows], axis=0).astype(bf16)
+    with jax.named_scope("E_straight"):
+        l_cv.wait()
+        straight = jnp.concatenate(
+            [dot(base, cv_v[...]), dot_nt(base, folded_high) + dot_nt(base, folded_low)], axis=1
+        )
+        straight_high = straight.astype(bf16)
+        straight_ref[:LANES] = straight_high
+        straight_ref[LANES:] = (straight - straight_high.astype(f32)).astype(bf16)
+        row_id = lax.broadcasted_iota(jnp.int32, (levels * rows, LANES), 0)
+        lane_id = lax.broadcasted_iota(jnp.int32, (levels * rows, LANES), 1)
+        marks = jnp.zeros((levels * rows, LANES), f32)
+        for l in range(levels):
+            inside = jnp.logical_and(row_id >= l * rows, row_id < (l + 1) * rows)
+            marks = jnp.where(jnp.logical_and(inside, lane_id == pixels + l), 1.0, marks)
+        slot = lax.rem(lax.broadcasted_iota(jnp.int32, (2 * LANES, channels), 0), LANES)
+        lane = lax.broadcasted_iota(jnp.int32, (2 * LANES, channels), 1) // head
+        for q in range(latents):
+            widen_ref[q] = jnp.where(slot == lane + q * HEADS, 1.0, 0.0).astype(bf16)
+
+    with jax.named_scope("H_zero"):
+        @pl.when(jnp.logical_not(has_low))
+        def _():
+            gathered[0] = jnp.zeros(gathered.shape[1:], bf16)
+
+        @pl.when(jnp.logical_not(has_high))
+        def _():
+            gathered[2] = jnp.zeros(gathered.shape[1:], bf16)
+
+    with jax.named_scope("HR_ready"):
+        @pl.when(has_high)
+        def _():
+            pl.semaphore_wait(ready_sem, var_count)
+            for d in range(var_count - 1, -1, -1):
+                send(d, 1).start()
+
+    with jax.named_scope("I_arrive1"):
+        own.wait()
+        used = latents * SHIFT * cols
+        for w in range(2):
+            if used < base_ref.shape[0] // 2:
+                fill = (base_ref.shape[0] // 2) * w + used
+                ask_ref[fill : (base_ref.shape[0] // 2) * (w + 1)] = jnp.zeros((base_ref.shape[0] // 2 - used, channels), f32)
+                base_ref[fill : (base_ref.shape[0] // 2) * (w + 1)] = jnp.zeros((base_ref.shape[0] // 2 - used, channels), f32)
+        for d in range(1, var_count):
+            arrival(d, 1).wait_recv()
+    with jax.named_scope("J_waitco"):
+        l_co.wait()
+        l_gain1.wait()
     grid = tall * cols
     block = rows * cols
     edge = SHIFT * cols
@@ -251,14 +280,16 @@
         for i in range(level_here):
             at = (v * level_here + i) * rows
             rows_ref[at : at + rows] = gathered[1, v, i].astype(f32)
-    l_wc.wait()
-    l_wq.wait()
+    with jax.named_scope("K_waitwc"):
+        l_wc.wait()
+        l_wq.wait()
     window = WLAT * cols
     half = SHIFT * cols
-    own_latent = jnp.concatenate(pool(), axis=0)
-    own_normed = layer_norm(own_latent, gain1_v[...]).astype(bf16)
-    context = dot(own_normed, wc_v[...])
-    asked = dot(own_normed, wq_v[...]) * (head ** (-0.5) * math.log2(math.e))
+    with jax.named_scope("L_ownpool"):
+        own_latent = jnp.concatenate(pool(), axis=0)
+        own_normed = layer_norm(own_latent, gain1_v[...]).astype(bf16)
+        context = dot(own_normed, wc_v[...])
+        asked = dot(own_normed, wq_v[...]) * (head ** (-0.5) * math.log2(math.e))
     part = half
     for q in range(latents):
         for w in range(2):
@@ -285,51 +316,60 @@
             at = (v * level_here + i) * rows
             rows_ref[at : at + SHIFT] = gathered[0, v, i].astype(f32)[rows - SHIFT :]
             rows_ref[at + SHIFT : at + rows] = gathered[2, v, i].astype(f32)[:SHIFT]
-    outer = pool()
-    edge_normed = layer_norm(jnp.concatenate(outer, axis=0), gain1_v[...])
-    edge_context = dot(edge_normed.astype(bf16), wc_v[...])
-    for q in range(latents):
-        at = q * block
+    with jax.named_scope("N_edgepool"):
+        outer = pool()
+    with jax.named_scope("O_edgectx"):
+        edge_normed = layer_norm(jnp.concatenate(outer, axis=0), gain1_v[...])
+        edge_context = dot(edge_normed.astype(bf16), wc_v[...])
+        for q in range(latents):
+            at = q * block
+            for w in range(2):
+                to = (w * latents + q) * window + w * half
+                key_ref[to : to + half] = edge_context[at + w * edge : at + (w + 1) * edge, :channels]
+                val_ref[to : to + half] = edge_context[at + w * edge : at + (w + 1) * edge, channels:]
+
+    with jax.named_scope("P_attn"):
+        span = latents * window
+        group = LANES // head
+        place = lax.rem(lax.broadcasted_iota(jnp.int32, (1, span), 1), window)
+        lane_of = lax.broadcasted_iota(jnp.int32, (count, LANES), 1) // head
+        empty = (
+            jnp.logical_and(place < half, jnp.logical_not(has_low)),
+            jnp.logical_and(place >= half, jnp.logical_not(has_high)),
+        )
         for w in range(2):
-            to = (w * latents + q) * window + w * half
-            key_ref[to : to + half] = edge_context[at + w * edge : at + (w + 1) * edge, :channels]
-            val_ref[to : to + half] = edge_context[at + w * edge : at + (w + 1) * edge, channels:]
-
-    span = latents * window
-    group = LANES // head
-    place = lax.rem(lax.broadcasted_iota(jnp.int32, (1, span), 1), window)
-    lane_of = lax.broadcasted_iota(jnp.int32, (count, LANES), 1) // head
-    empty = (
-        jnp.logical_and(place < half, jnp.logical_not(has_low)),
-        jnp.logical_and(place >= half, jnp.logical_not(has_high)),
-    )
-    for w in range(2):
-        offset = jnp.where(empty[w], masked_score, 0.0)
-        for g in range(channels // LANES):
-            lanes = slice(g * LANES, (g + 1) * LANES)
-            ask = ask_ref[w * count : (w + 1) * count, lanes]
-            keys = key_ref[w * span : (w + 1) * span, lanes].astype(bf16)
-            vals = val_ref[w * span : (w + 1) * span, lanes].astype(bf16)
-            asks = jnp.concatenate(
-                [jnp.where(lane_of == h, ask, 0.0) for h in range(group)], axis=0
-            ).astype(bf16)
-            logits = dot_nt(asks, keys) + offset
-            power = jnp.exp2(logits - jnp.max(logits, axis=-1, keepdims=True))
-            amount = jnp.sum(power, axis=-1, keepdims=True)
-            taken = dot(power.astype(bf16), vals) / amount
-            joined = taken[:count]
-            for h in range(1, group):
-                joined = jnp.where(lane_of == h, taken[h * count : (h + 1) * count], joined)
-            mix_ref[w * count : (w + 1) * count, lanes] = joined
-
-    l_wo.wait()
-    l_gain2.wait()
-    mixed = dot(mix_ref[...].astype(bf16), wo_v[...]) + base_ref[...]
-    second = layer_norm(mixed, gain2_v[...]).astype(bf16)
-    l_up.wait()
-    hidden = jax.nn.gelu(dot(second, up_v[...])).astype(bf16)
-    l_down.wait()
-    res_ref[...] = mixed + dot(hidden, down_v[...])
+            offset = jnp.where(empty[w], masked_score, 0.0)
+            for g in range(channels // LANES):
+                lanes = slice(g * LANES, (g + 1) * LANES)
+                ask = ask_ref[w * count : (w + 1) * count, lanes]
+                keys = key_ref[w * span : (w + 1) * span, lanes].astype(bf16)
+                vals = val_ref[w * span : (w + 1) * span, lanes].astype(bf16)
+                asks = jnp.concatenate(
+                    [jnp.where(lane_of == h, ask, 0.0) for h in range(group)], axis=0
+                ).astype(bf16)
+                logits = dot_nt(asks, keys) + offset
+                power = jnp.exp2(logits - jnp.max(logits, axis=-1, keepdims=True))
+                amount = jnp.sum(power, axis=-1, keepdims=True)
+                taken = dot(power.astype(bf16), vals) / amount
+                joined = taken[:count]
+                for h in range(1, group):
+                    joined = jnp.where(lane_of == h, taken[h * count : (h + 1) * count], joined)
+                mix_ref[w * count : (w + 1) * count, lanes] = joined
+
+    with jax.named_scope("Q_waitwo"):
+        l_wo.wait()
+        l_gain2.wait()
+    with jax.named_scope("R_wo"):
+        mixed = dot(mix_ref[...].astype(bf16), wo_v[...]) + base_ref[...]
+        second = layer_norm(mixed, gain2_v[...]).astype(bf16)
+    with jax.named_scope("S_waitup"):
+        l_up.wait()
+    with jax.named_scope("T_up"):
+        hidden = jax.nn.gelu(dot(second, up_v[...])).astype(bf16)
+    with jax.named_scope("U_waitdown"):
+        l_down.wait()
+    with jax.named_scope("V_down"):
+        res_ref[...] = mixed + dot(hidden, down_v[...])
     for d in range(1, var_count):
         send(d, 0).wait_send()
 
@@ -402,6 +442,7 @@
                 pltpu.SemaphoreType.DMA((len(operands) + 1,)),
                 pltpu.SemaphoreType.DMA((3, var_count)),
                 pltpu.SemaphoreType.DMA((3, var_count)),
+                pltpu.SemaphoreType.REGULAR,
             ],
             compiler_params=pltpu.CompilerParams(collective_id=0, has_side_effects=True,
                                                  vmem_limit_bytes=36 * 1024 * 1024),

time: 15.6 us -> 14.5 us (0.929)
  Pallas kernels: 15.4 us -> 14.3 us
    pallas_call x1, Pallas kernels: 14.7 us -> 13.6 us  [body(): pl.pallas_call(functools.partial(kernel, sizes), out_shape=jax.ShapeDtype...]
where the time goes in v1:
time: 14.5 us; the launch traced here: 14.3 us
  Pallas kernels  14.3 us (99%)
    pallas_call x1, Pallas kernels, body(): pl.pallas_call(functools.partial(kernel, sizes), out_shape=jax.ShapeDtype...  13.6 us
    pallas_call x1, Pallas kernels, body(): pl.pallas_call(functools.partial(finish, (latents, cols, SHIFT * cols, co...  0.75 us

profile of v1, /device:TPU:0, one launch (start us, length us, event | category | flops | bytes accessed | tf_op | source)
XLA Modules:
  0.0 14.3 jit_solution(2684011939974238584)
XLA Ops:
  0.0 13.6 %shard_map.136.res_ref = f32[224,512]{1,0:T(8,128)S(1)} custom-call(bf16[1,6,3840]{2,1,0:T(8,128)(2,1)} %patches_hbm.1, bf16[4,512]{1,0:T(4,128)(2,1)} %bias_hbm.1, bf16[80,512]{1,0:T(8,128)(2,1)} %embed_hbm.1, bf16[3,512]{1,0:T(4,128)(2,1)} %query_hbm.1, bf16[512,512]{1,0:T(8,128)(2,1)} %ck_hbm.1, bf16[512,512]{1,0:T(8,128)(2,1)} %cv_hbm.1, ...), custom_call_target="tpu_custom_call" | custom-call | tf_op jit(solution)/shard_map/pallas_call | solution.py:423
  13.6 0.8 %shard_map.137 = bf16[3,6,12,512]{3,2,1,0:T(8,128)(2,1)} custom-call(f32[224,512]{1,0:T(8,128)S(1)} %shard_map.136.res_ref), custom_call_target="tpu_custom_call" | custom-call | tf_op jit(solution)/shard_map/pallas_call | solution.py:450

commit v2 on v1

--- a/solution.py
+++ b/solution.py
@@ -39,6 +39,12 @@
 
 def dot_nt(a, b):
     return lax.dot_general(a, b, (((1,), (1,)), ((), ())), preferred_element_type=f32)
+
+
+def gelu_twice(raw):
+    flat = raw.astype(bf16)
+    inner = flat * (flat * flat * bf16(0.044715 * math.sqrt(2.0 / math.pi)) + bf16(math.sqrt(2.0 / math.pi)))
+    return flat * (jnp.tanh(inner) + bf16(1.0)) * bf16(0.5)
 
 
 def kernel(
@@ -49,7 +55,7 @@
     patches_v, gathered, rows_ref, bias_v, embed_v, query_v, ck_v, cv_v, co_v, gain1_v,
     wq_v, wc_v, wo_v, gain2_v, up_v, down_v,
     straight_ref, widen_ref, token_ref, value_ref, key_ref, val_ref, ask_ref, base_ref, mix_ref,
-    load_sem, send_sem, recv_sem, ready_sem,
+    recv_sem, ready_sem, load_sem, send_sem,
 ):
     var_count, lat_count, level_here, rows, cols, pixels, width, channels, latents = sizes
     levels = var_count * level_here
@@ -128,19 +134,19 @@
             src_ref=patches_v.at[:, :, pl.ds(start_of(target), width)],
             dst_ref=gathered.at[1 - step, me],
             send_sem=send_sem.at[1 - step, d],
-            recv_sem=recv_sem.at[1 - step, me],
+            recv_sem=recv_sem.at[1 - step],
             device_id={"var": target, "lat": band + step},
             device_id_type=MESH,
         )
 
-    def arrival(d, slot):
-        source = peer(d)
+    def arrivals(slot, amount):
+        together = gathered.at[slot, pl.ds(0, amount)]
         return pltpu.make_async_remote_copy(
-            src_ref=patches_v.at[:, :, pl.ds(start_of(me), width)],
-            dst_ref=gathered.at[slot, source],
-            send_sem=send_sem.at[slot, d],
-            recv_sem=recv_sem.at[slot, source],
-            device_id={"var": source, "lat": band},
+            src_ref=together,
+            dst_ref=together,
+            send_sem=send_sem.at[slot, 0],
+            recv_sem=recv_sem.at[slot],
+            device_id={"var": me, "lat": band},
             device_id_type=MESH,
         )
 
@@ -227,8 +233,7 @@
                 fill = (base_ref.shape[0] // 2) * w + used
                 ask_ref[fill : (base_ref.shape[0] // 2) * (w + 1)] = jnp.zeros((base_ref.shape[0] // 2 - used, channels), f32)
                 base_ref[fill : (base_ref.shape[0] // 2) * (w + 1)] = jnp.zeros((base_ref.shape[0] // 2 - used, channels), f32)
-        for d in range(1, var_count):
-            arrival(d, 1).wait_recv()
+        arrivals(1, var_count - 1).wait_recv()
     with jax.named_scope("J_waitco"):
         l_co.wait()
         l_gain1.wait()
@@ -252,21 +257,23 @@
             )
         tokens = token_ref[...].astype(bf16)
         made = dot(jnp.concatenate([tokens, tokens], axis=1), straight_ref[...])
-        value_ref[...] = made[:, :channels]
+        value_ref[:block] = made[:block, :channels]
+        for at in range(block, levels * block, block):
+            value_ref[at : at + block] = made[at : at + block, :channels] - made[:block, :channels]
         scores = made[:, channels:]
         pieces = [scores[l * block : (l + 1) * block] for l in range(levels)]
         highest = functools.reduce(jnp.maximum, pieces)
         weights = [jnp.exp2(piece - highest) for piece in pieces]
         inverse = 1.0 / functools.reduce(jnp.add, weights)
-        share = jnp.concatenate([weight * inverse for weight in weights], axis=0)
+        share = jnp.concatenate([weight * inverse for weight in weights[1:]], axis=0)
         high = share.astype(bf16)
         low = (share - high.astype(f32)).astype(bf16)
         shares = jnp.concatenate([high, low], axis=1)
         found = []
         for q in range(latents):
-            parts = dot(shares, widen_ref[q]) * value_ref[...]
+            parts = dot(shares, widen_ref[q]) * value_ref[block:]
             total = functools.reduce(
-                jnp.add, [parts[l * block : (l + 1) * block] for l in range(levels)]
+                jnp.add, [parts[l * block : (l + 1) * block] for l in range(levels - 1)], value_ref[:block]
             )
             found.append(total)
         joined = dot(jnp.concatenate(found, axis=0).astype(bf16), co_v[...])
@@ -303,13 +310,11 @@
 
     @pl.when(has_low)
     def _():
-        for d in range(var_count):
-            arrival(d, 0).wait_recv()
+        arrivals(0, var_count).wait_recv()
 
     @pl.when(has_high)
     def _():
-        for d in range(var_count):
-            arrival(d, 2).wait_recv()
+        arrivals(2, var_count).wait_recv()
 
     for v in range(var_count):
         for i in range(level_here):
@@ -328,6 +333,11 @@
                 key_ref[to : to + half] = edge_context[at + w * edge : at + (w + 1) * edge, :channels]
                 val_ref[to : to + half] = edge_context[at + w * edge : at + (w + 1) * edge, channels:]
 
+    with jax.named_scope("Q_wait"):
+        l_wo.wait()
+        l_gain2.wait()
+        l_up.wait()
+        l_down.wait()
     with jax.named_scope("P_attn"):
         span = latents * window
         group = LANES // head
@@ -356,20 +366,16 @@
                     joined = jnp.where(lane_of == h, taken[h * count : (h + 1) * count], joined)
                 mix_ref[w * count : (w + 1) * count, lanes] = joined
 
-    with jax.named_scope("Q_waitwo"):
-        l_wo.wait()
-        l_gain2.wait()
     with jax.named_scope("R_wo"):
         mixed = dot(mix_ref[...].astype(bf16), wo_v[...]) + base_ref[...]
         second = layer_norm(mixed, gain2_v[...]).astype(bf16)
-    with jax.named_scope("S_waitup"):
-        l_up.wait()
-    with jax.named_scope("T_up"):
-        hidden = jax.nn.gelu(dot(second, up_v[...])).astype(bf16)
-    with jax.named_scope("U_waitdown"):
-        l_down.wait()
-    with jax.named_scope("V_down"):
-        res_ref[...] = mixed + dot(hidden, down_v[...])
+    with jax.named_scope("T_mlp"):
+        units = up_v.shape[1]
+        chunk = 512
+        total = mixed
+        waiting = None
+        hidden = [gelu_twice(dot(second, up_v[:, c : c + chunk])) for c in range(0, units, chunk)]
+        res_ref[...] = mixed + dot(jnp.concatenate(hidden, axis=1), down_v[...])
     for d in range(1, var_count):
         send(d, 0).wait_send()
 
@@ -382,6 +388,15 @@
     def _():
         for d in range(var_count):
             send(d, 1).wait_send()
+
+
+def launch(sizes, *refs):
+    def run(load_sem, send_sem):
+        kernel(sizes, *refs, load_sem, send_sem)
+
+    pl.run_scoped(
+        run, pltpu.SemaphoreType.DMA((16,)), pltpu.SemaphoreType.DMA((3, sizes[0]))
+    )
 
 
 def finish(sizes, res_ref, out_ref):
@@ -421,7 +436,7 @@
         any_spec = pl.BlockSpec(memory_space=pl.ANY)
         weights = [pltpu.VMEM(x.shape, x.dtype) for x in operands[1:]]
         result = pl.pallas_call(
-            functools.partial(kernel, sizes),
+            functools.partial(launch, sizes),
             out_shape=jax.ShapeDtypeStruct((2 * count, channels), f32),
             in_specs=[any_spec] * len(operands),
             out_specs=pl.BlockSpec(memory_space=pltpu.VMEM),
@@ -439,9 +454,7 @@
                 pltpu.VMEM((2 * count, channels), f32),
                 pltpu.VMEM((2 * count, channels), f32),
                 pltpu.VMEM((2 * count, channels), f32),
-                pltpu.SemaphoreType.DMA((len(operands) + 1,)),
-                pltpu.SemaphoreType.DMA((3, var_count)),
-                pltpu.SemaphoreType.DMA((3, var_count)),
+                pltpu.SemaphoreType.DMA((3,)),
                 pltpu.SemaphoreType.REGULAR,
             ],
             compiler_params=pltpu.CompilerParams(collective_id=0, has_side_effects=True,

time: 14.5 us -> 13.5 us (0.931)
  Pallas kernels: 14.3 us -> 13.4 us
    pallas_call x1, Pallas kernels: 13.6 us -> 12.6 us  [body(): pl.pallas_call(functools.partial(launch, sizes), out_shape=jax.ShapeDtype...]
where the time goes in v2:
time: 13.5 us; the launch traced here: 13.4 us
  Pallas kernels  13.4 us (99%)
    pallas_call x1, Pallas kernels, body(): pl.pallas_call(functools.partial(launch, sizes), out_shape=jax.ShapeDtype...  12.6 us
    pallas_call x1, Pallas kernels, body(): pl.pallas_call(functools.partial(finish, (latents, cols, SHIFT * cols, co...  0.75 us

profile of v2, /device:TPU:0, one launch (start us, length us, event | category | flops | bytes accessed | tf_op | source)
XLA Modules:
  0.0 13.4 jit_solution(2995018496543090562)
XLA Ops:
  0.0 12.6 %shard_map.136.res_ref = f32[224,512]{1,0:T(8,128)S(1)} custom-call(bf16[1,6,3840]{2,1,0:T(8,128)(2,1)} %refs_0_.1, bf16[4,512]{1,0:T(4,128)(2,1)} %refs_1_.1, bf16[80,512]{1,0:T(8,128)(2,1)} %refs_2_.1, bf16[3,512]{1,0:T(4,128)(2,1)} %refs_3_.1, bf16[512,512]{1,0:T(8,128)(2,1)} %refs_4_.1, bf16[512,512]{1,0:T(8,128)(2,1)} %refs_5_.1, ...), custom_call_target="tpu_custom_call" | custom-call | tf_op jit(solution)/shard_map/pallas_call | solution.py:438
  12.6 0.8 %shard_map.137 = bf16[3,6,12,512]{3,2,1,0:T(8,128)(2,1)} custom-call(f32[224,512]{1,0:T(8,128)S(1)} %shard_map.136.res_ref), custom_call_target="tpu_custom_call" | custom-call | tf_op jit(solution)/shard_map/pallas_call | solution.py:463

commit v3 on v2

--- a/solution.py
+++ b/solution.py
@@ -54,7 +54,7 @@
     res_ref,
     patches_v, gathered, rows_ref, bias_v, embed_v, query_v, ck_v, cv_v, co_v, gain1_v,
     wq_v, wc_v, wo_v, gain2_v, up_v, down_v,
-    straight_ref, widen_ref, token_ref, value_ref, key_ref, val_ref, ask_ref, base_ref, mix_ref,
+    straight_ref, widen_ref, token_ref, value_ref, key_ref, val_ref, turned_ref, ask_ref, base_ref, mix_ref,
     recv_sem, ready_sem, load_sem, send_sem,
 ):
     var_count, lat_count, level_here, rows, cols, pixels, width, channels, latents = sizes
@@ -218,6 +218,15 @@
         def _():
             gathered[2] = jnp.zeros(gathered.shape[1:], bf16)
 
+    count = round_up(latents * SHIFT * cols, 2 * SUBLANES)
+    span = 2 * LANES
+    filled = latents * SHIFT * cols
+    for w in range(2):
+        for start, end in ((filled, count), (count + filled, span)):
+            key_ref[w * span + start : w * span + end] = jnp.zeros((end - start, channels), f32)
+            val_ref[w * span + start : w * span + end] = jnp.zeros((end - start, channels), f32)
+        ask_ref[w * LANES + filled : (w + 1) * LANES] = jnp.zeros((LANES - filled, channels), f32)
+
     with jax.named_scope("HR_ready"):
         @pl.when(has_high)
         def _():
@@ -231,7 +240,6 @@
         for w in range(2):
             if used < base_ref.shape[0] // 2:
                 fill = (base_ref.shape[0] // 2) * w + used
-                ask_ref[fill : (base_ref.shape[0] // 2) * (w + 1)] = jnp.zeros((base_ref.shape[0] // 2 - used, channels), f32)
                 base_ref[fill : (base_ref.shape[0] // 2) * (w + 1)] = jnp.zeros((base_ref.shape[0] // 2 - used, channels), f32)
         arrivals(1, var_count - 1).wait_recv()
     with jax.named_scope("J_waitco"):
@@ -282,7 +290,6 @@
             for q in range(latents)
         ]
 
-    count = round_up(latents * SHIFT * cols, SUBLANES)
     for v in range(var_count):
         for i in range(level_here):
             at = (v * level_here + i) * rows
@@ -301,11 +308,12 @@
     for q in range(latents):
         for w in range(2):
             at = q * block + w * half
-            to = (w * latents + q) * window + (1 - w) * half
+            to = w * span + q * half
             key_ref[to : to + half] = context[at : at + half, :channels]
             val_ref[to : to + half] = context[at : at + half, channels:]
+            to = w * LANES + q * half
+            ask_ref[to : to + half] = asked[at : at + half]
             to = w * count + q * half
-            ask_ref[to : to + half] = asked[at : at + half]
             base_ref[to : to + half] = own_latent[at : at + half]
 
     @pl.when(has_low)
@@ -329,7 +337,7 @@
         for q in range(latents):
             at = q * block
             for w in range(2):
-                to = (w * latents + q) * window + w * half
+                to = w * span + count + q * half
                 key_ref[to : to + half] = edge_context[at + w * edge : at + (w + 1) * edge, :channels]
                 val_ref[to : to + half] = edge_context[at + w * edge : at + (w + 1) * edge, channels:]
 
@@ -339,35 +347,57 @@
         l_up.wait()
         l_down.wait()
     with jax.named_scope("P_attn"):
-        span = latents * window
         group = LANES // head
-        place = lax.rem(lax.broadcasted_iota(jnp.int32, (1, span), 1), window)
-        lane_of = lax.broadcasted_iota(jnp.int32, (count, LANES), 1) // head
-        empty = (
-            jnp.logical_and(place < half, jnp.logical_not(has_low)),
-            jnp.logical_and(place >= half, jnp.logical_not(has_high)),
-        )
+        kept = 2 * count
+        place = lax.broadcasted_iota(jnp.int32, (kept, LANES), 0)
+        filler = lax.rem(place, count) >= latents * half
+        missing = (jnp.logical_not(has_low), jnp.logical_not(has_high))
+        nothing = jnp.zeros((head, LANES), bf16)
+        ones = jnp.ones((2 * SUBLANES, kept), bf16)
+        asks, offsets = [], []
         for w in range(2):
-            offset = jnp.where(empty[w], masked_score, 0.0)
-            for g in range(channels // LANES):
-                lanes = slice(g * LANES, (g + 1) * LANES)
-                ask = ask_ref[w * count : (w + 1) * count, lanes]
-                keys = key_ref[w * span : (w + 1) * span, lanes].astype(bf16)
-                vals = val_ref[w * span : (w + 1) * span, lanes].astype(bf16)
-                asks = jnp.concatenate(
-                    [jnp.where(lane_of == h, ask, 0.0) for h in range(group)], axis=0
+            empty = jnp.logical_or(filler, jnp.logical_and(place >= count, missing[w]))
+            offsets.append(jnp.where(empty, masked_score, 0.0))
+            turned_ref[:, w * span : (w + 1) * span] = val_ref[w * span : (w + 1) * span].astype(bf16).T
+            asks.append(ask_ref[w * LANES : (w + 1) * LANES].astype(bf16).T)
+
+        def score(w, g, p):
+            keys = key_ref[w * span : w * span + kept, g * LANES : (g + 1) * LANES].astype(bf16)
+            at = (g * group + p) * head
+            sides = []
+            for side in range(2):
+                tiles = [nothing] * group
+                tiles[p + side] = asks[w][at + side * head : at + (side + 1) * head]
+                sides.append(jnp.concatenate(tiles, axis=0))
+            return dot(keys, jnp.concatenate(sides, axis=1)) + jnp.concatenate([offsets[w]] * 2, axis=1)
+
+        def power_of(logits):
+            top = functools.reduce(jnp.maximum, [logits[i : i + 56] for i in range(0, kept, 56)])
+            return jnp.exp2((logits - jnp.max(top, axis=0, keepdims=True)).astype(bf16))
+
+        def take(w, g, p, power):
+            at = (g * group + p) * head
+            vals = jnp.concatenate([turned_ref[at : at + 2 * head, w * span : w * span + kept], ones], axis=0)
+            taken = dot(vals, power)
+            amount = 1.0 / taken[2 * head : 2 * head + 1]
+            for side in range(2):
+                tile = slice(side * LANES, (side + 1) * LANES)
+                rows_at = slice(side * head, (side + 1) * head)
+                mix_ref[at + side * head : at + (side + 1) * head, w * LANES : (w + 1) * LANES] = (
+                    taken[rows_at, tile] * amount[:, tile]
                 ).astype(bf16)
-                logits = dot_nt(asks, keys) + offset
-                power = jnp.exp2(logits - jnp.max(logits, axis=-1, keepdims=True))
-                amount = jnp.sum(power, axis=-1, keepdims=True)
-                taken = dot(power.astype(bf16), vals) / amount
-                joined = taken[:count]
-                for h in range(1, group):
-                    joined = jnp.where(lane_of == h, taken[h * count : (h + 1) * count], joined)
-                mix_ref[w * count : (w + 1) * count, lanes] = joined
+
+        turns = [(w, g, p) for w in range(2) for g in range(channels // LANES) for p in range(0, group, 2)]
+        scored = {}
+        for i in range(len(turns) + 16):
+            if i < len(turns):
+                scored[i] = power_of(score(*turns[i]))
+            if i >= 16:
+                take(*turns[i - 16], scored.pop(i - 16))
 
     with jax.named_scope("R_wo"):
-        mixed = dot(mix_ref[...].astype(bf16), wo_v[...]) + base_ref[...]
+        mixes = [mix_ref[:, w * LANES : (w + 1) * LANES].T[:count] for w in range(2)]
+        mixed = dot(jnp.concatenate(mixes, axis=0), wo_v[...]) + base_ref[...]
         second = layer_norm(mixed, gain2_v[...]).astype(bf16)
     with jax.named_scope("T_mlp"):
         units = up_v.shape[1]
@@ -422,12 +452,12 @@
         cols = flat // pixels // var_count
         levels = level_here * var_count
         assert rows == WLAT == 2 * SHIFT and cols == WLON
-        assert pixels + levels <= LANES >= latents * HEADS
+        count = round_up(latents * SHIFT * cols, 2 * SUBLANES)
+        assert pixels + levels <= LANES >= max(latents * HEADS, count)
         width = round_up(cols * pixels + max(v * cols * pixels % LANES for v in range(var_count)), LANES)
         tall = rows + 2 * SHIFT
         grid = tall * cols
-        span = latents * WLAT * cols
-        count = round_up(latents * SHIFT * cols, SUBLANES)
+        count = round_up(latents * SHIFT * cols, 2 * SUBLANES)
         sizes = (var_count, lat_count, level_here, rows, cols, pixels, width, channels, latents)
         operands = list(args)
         operands[7] = first_gain.reshape(1, channels)
@@ -449,11 +479,12 @@
                 pltpu.VMEM((latents, 2 * LANES, channels), bf16),
                 pltpu.VMEM((levels * rows * cols, LANES), f32),
                 pltpu.VMEM((levels * rows * cols, channels), f32),
-                pltpu.VMEM((2 * span, channels), f32),
-                pltpu.VMEM((2 * span, channels), f32),
+                pltpu.VMEM((4 * LANES, channels), f32),
+                pltpu.VMEM((4 * LANES, channels), f32),
+                pltpu.VMEM((channels, 4 * LANES), bf16),
+                pltpu.VMEM((2 * LANES, channels), f32),
                 pltpu.VMEM((2 * count, channels), f32),
-                pltpu.VMEM((2 * count, channels), f32),
-                pltpu.VMEM((2 * count, channels), f32),
+                pltpu.VMEM((channels, 2 * LANES), bf16),
                 pltpu.SemaphoreType.DMA((3,)),
                 pltpu.SemaphoreType.REGULAR,
             ],

time: 13.5 us -> 13.4 us (level)
  Pallas kernels: 13.4 us -> 13.2 us
    pallas_call x1, Pallas kernels: 12.6 us -> 12.5 us  [body(): pl.pallas_call(functools.partial(launch, sizes), out_shape=jax.ShapeDtype...]
where the time goes in v3:
time: 13.4 us; the launch traced here: 13.2 us
  Pallas kernels  13.2 us (99%)
    pallas_call x1, Pallas kernels, body(): pl.pallas_call(functools.partial(launch, sizes), out_shape=jax.ShapeDtype...  12.5 us
    pallas_call x1, Pallas kernels, body(): pl.pallas_call(functools.partial(finish, (latents, cols, SHIFT * cols, co...  0.75 us

profile of v3, /device:TPU:0, one launch (start us, length us, event | category | flops | bytes accessed | tf_op | source)
XLA Modules:
  0.0 13.2 jit_solution(2126933046015149622)
XLA Ops:
  0.0 12.5 %shard_map.136.res_ref = f32[224,512]{1,0:T(8,128)S(1)} custom-call(bf16[1,6,3840]{2,1,0:T(8,128)(2,1)} %refs_0_.1, bf16[4,512]{1,0:T(4,128)(2,1)} %refs_1_.1, bf16[80,512]{1,0:T(8,128)(2,1)} %refs_2_.1, bf16[3,512]{1,0:T(4,128)(2,1)} %refs_3_.1, bf16[512,512]{1,0:T(8,128)(2,1)} %refs_4_.1, bf16[512,512]{1,0:T(8,128)(2,1)} %refs_5_.1, ...), custom_call_target="tpu_custom_call" | custom-call | tf_op jit(solution)/shard_map/pallas_call | solution.py:468
  12.5 0.8 %shard_map.137 = bf16[3,6,12,512]{3,2,1,0:T(8,128)(2,1)} custom-call(f32[224,512]{1,0:T(8,128)S(1)} %shard_map.136.res_ref), custom_call_target="tpu_custom_call" | custom-call | tf_op jit(solution)/shard_map/pallas_call | solution.py:494

commit v4 on v3

--- a/solution.py
+++ b/solution.py
@@ -52,7 +52,7 @@
     patches_hbm, bias_hbm, embed_hbm, query_hbm, ck_hbm, cv_hbm, co_hbm, gain1_hbm,
     wq_hbm, wc_hbm, wo_hbm, gain2_hbm, up_hbm, down_hbm,
     res_ref,
-    patches_v, gathered, rows_ref, bias_v, embed_v, query_v, ck_v, cv_v, co_v, gain1_v,
+    staged, gathered, rows_ref, bias_v, embed_v, query_v, ck_v, cv_v, co_v, gain1_v,
     wq_v, wc_v, wo_v, gain2_v, up_v, down_v,
     straight_ref, widen_ref, token_ref, value_ref, key_ref, val_ref, turned_ref, ask_ref, base_ref, mix_ref,
     recv_sem, ready_sem, load_sem, send_sem,
@@ -110,14 +110,14 @@
     def start_of(var):
         return pl.multiple_of(var * (cols * pixels) // LANES * LANES, LANES)
 
-    own = pltpu.make_async_copy(
-        patches_hbm.at[:, :, pl.ds(start_of(me), width)], gathered.at[1, me], load_sem.at[len(pairs)]
-    )
-    own.start()
-    stage = pltpu.make_async_copy(patches_hbm, patches_v, load_sem.at[len(pairs) + 1])
-    stage.start()
-    for load in loads[:5]:
-        load.start()
+    stages = {}
+    for d in range(var_count - 1, -1, -1):
+        stages[d] = pltpu.make_async_copy(
+            patches_hbm.at[:, :, pl.ds(start_of(peer(d)), width)],
+            staged.at[d] if d else gathered.at[1, me],
+            load_sem.at[len(pairs) + d],
+        )
+        stages[d].start()
 
     with jax.named_scope("F_barrier"):
         pl.semaphore_wait(
@@ -125,13 +125,11 @@
             var_count - 1 + var_count * has_low.astype(jnp.int32),
         )
 
-    with jax.named_scope("G_stage"):
-        stage.wait()
 
     def send(d, step):
         target = peer(d)
         return pltpu.make_async_remote_copy(
-            src_ref=patches_v.at[:, :, pl.ds(start_of(target), width)],
+            src_ref=staged.at[d] if d else gathered.at[1, me],
             dst_ref=gathered.at[1 - step, me],
             send_sem=send_sem.at[1 - step, d],
             recv_sem=recv_sem.at[1 - step],
@@ -150,17 +148,27 @@
             device_id_type=MESH,
         )
 
+    for load in loads[:5]:
+        load.start()
+
     for d in range(var_count - 1, 0, -1):
+        with jax.named_scope("G_stage"):
+            stages[d].wait()
         send(d, 0).start()
 
     @pl.when(has_low)
     def _():
-        for d in range(var_count):
-            pl.semaphore_signal(
-                ready_sem, inc=1, device_id={"var": peer(d), "lat": band - 1}, device_id_type=MESH
-            )
-        for d in range(var_count - 1, -1, -1):
+        pl.semaphore_signal(
+            ready_sem, inc=1, device_id={"var": me, "lat": band - 1}, device_id_type=MESH
+        )
+        for d in range(var_count - 1, 0, -1):
             send(d, -1).start()
+
+    stages[0].wait()
+
+    @pl.when(has_low)
+    def _():
+        send(0, -1).start()
 
     with jax.named_scope("H_startloads"):
         for load in loads[5:]:
@@ -230,12 +238,11 @@
     with jax.named_scope("HR_ready"):
         @pl.when(has_high)
         def _():
-            pl.semaphore_wait(ready_sem, var_count)
+            pl.semaphore_wait(ready_sem, 1)
             for d in range(var_count - 1, -1, -1):
                 send(d, 1).start()
 
     with jax.named_scope("I_arrive1"):
-        own.wait()
         used = latents * SHIFT * cols
         for w in range(2):
             if used < base_ref.shape[0] // 2:
@@ -355,9 +362,10 @@
         nothing = jnp.zeros((head, LANES), bf16)
         ones = jnp.ones((2 * SUBLANES, kept), bf16)
         asks, offsets = [], []
+        sure = latents * half // SUBLANES * SUBLANES
         for w in range(2):
             empty = jnp.logical_or(filler, jnp.logical_and(place >= count, missing[w]))
-            offsets.append(jnp.where(empty, masked_score, 0.0))
+            offsets.append(jnp.where(empty, masked_score, 0.0)[sure:])
             turned_ref[:, w * span : (w + 1) * span] = val_ref[w * span : (w + 1) * span].astype(bf16).T
             asks.append(ask_ref[w * LANES : (w + 1) * LANES].astype(bf16).T)
 
@@ -369,7 +377,9 @@
                 tiles = [nothing] * group
                 tiles[p + side] = asks[w][at + side * head : at + (side + 1) * head]
                 sides.append(jnp.concatenate(tiles, axis=0))
-            return dot(keys, jnp.concatenate(sides, axis=1)) + jnp.concatenate([offsets[w]] * 2, axis=1)
+            logits = dot(keys, jnp.concatenate(sides, axis=1))
+            masked = logits[sure:] + jnp.concatenate([offsets[w]] * 2, axis=1)
+            return jnp.concatenate([logits[:sure], masked], axis=0)
 
         def power_of(logits):
             top = functools.reduce(jnp.maximum, [logits[i : i + 56] for i in range(0, kept, 56)])
@@ -425,17 +435,29 @@
         kernel(sizes, *refs, load_sem, send_sem)
 
     pl.run_scoped(
-        run, pltpu.SemaphoreType.DMA((16,)), pltpu.SemaphoreType.DMA((3, sizes[0]))
+        run, pltpu.SemaphoreType.DMA((13 + sizes[0],)), pltpu.SemaphoreType.DMA((3, sizes[0]))
     )
 
 
-def finish(sizes, res_ref, out_ref):
+def finish(sizes, res_ref, out_hbm, out_ref):
     latents, cols, part, count = sizes
-    for w in range(2):
-        for q in range(latents):
-            for r in range(SHIFT):
-                at = w * count + q * part + r * cols
-                out_ref[q, w * SHIFT + r] = res_ref[at : at + cols].astype(bf16)
+
+    def run(sems):
+        copies = []
+        for w in range(2):
+            for q in range(latents):
+                for r in range(SHIFT):
+                    at = w * count + q * part + r * cols
+                    out_ref[q, w * SHIFT + r] = res_ref[at : at + cols].astype(bf16)
+                piece = (q, pl.ds(w * SHIFT, SHIFT))
+                copies.append(pltpu.make_async_copy(
+                    out_ref.at[piece], out_hbm.at[piece], sems.at[w * latents + q]
+                ))
+                copies[-1].start()
+        for copy in copies:
+            copy.wait()
+
+    pl.run_scoped(run, pltpu.SemaphoreType.DMA((2 * latents,)))
 
 
 def solution(mesh):
@@ -471,7 +493,7 @@
             in_specs=[any_spec] * len(operands),
             out_specs=pl.BlockSpec(memory_space=pltpu.VMEM),
             scratch_shapes=[
-                pltpu.VMEM(args[0].shape, bf16),
+                pltpu.VMEM((var_count, level_here, rows, width), bf16),
                 pltpu.VMEM((3, var_count, level_here, rows, width), bf16),
                 pltpu.VMEM((levels * rows, width), f32),
                 *weights,
@@ -495,7 +517,8 @@
             functools.partial(finish, (latents, cols, SHIFT * cols, count)),
             out_shape=jax.ShapeDtypeStruct((latents, rows, cols, channels), bf16),
             in_specs=[pl.BlockSpec(memory_space=pltpu.VMEM)],
-            out_specs=pl.BlockSpec(memory_space=pltpu.VMEM),
+            out_specs=pl.BlockSpec(memory_space=pl.ANY),
+            scratch_shapes=[pltpu.VMEM((latents, rows, cols, channels), bf16)],
             compiler_params=pltpu.CompilerParams(vmem_limit_bytes=16 * 1024 * 1024),
         )(result)
 

time: 13.4 us -> 13.4 us (level)
  no operation moved by 1% of the time
where the time goes in v4:
time: 13.4 us; the launch traced here: 13.2 us
  Pallas kernels  13.2 us (99%)
    pallas_call x1, Pallas kernels, body(): pl.pallas_call(functools.partial(launch, sizes), out_shape=jax.ShapeDtype...  12.5 us
    pallas_call x1, Pallas kernels, body(): pl.pallas_call(functools.partial(finish, (latents, cols, SHIFT * cols, co...  0.71 us

profile of v4, /device:TPU:0, one launch (start us, length us, event | category | flops | bytes accessed | tf_op | source)
XLA Modules:
  0.0 13.2 jit_solution(6599596197005373241)
XLA Ops:
  0.0 12.5 %shard_map.136.res_ref = f32[224,512]{1,0:T(8,128)S(1)} custom-call(bf16[1,6,3840]{2,1,0:T(8,128)(2,1)} %refs_0_.1, bf16[4,512]{1,0:T(4,128)(2,1)} %refs_1_.1, bf16[80,512]{1,0:T(8,128)(2,1)} %refs_2_.1, bf16[3,512]{1,0:T(4,128)(2,1)} %refs_3_.1, bf16[512,512]{1,0:T(8,128)(2,1)} %refs_4_.1, bf16[512,512]{1,0:T(8,128)(2,1)} %refs_5_.1, ...), custom_call_target="tpu_custom_call" | custom-call | tf_op jit(solution)/shard_map/pallas_call | solution.py:490
  12.5 0.7 %shard_map.137 = bf16[3,6,12,512]{3,2,1,0:T(8,128)(2,1)} custom-call(f32[224,512]{1,0:T(8,128)S(1)} %shard_map.136.res_ref), custom_call_target="tpu_custom_call" | custom-call | tf_op jit(solution)/shard_map/pallas_call | solution.py:516

commit v5 on v4

--- a/solution.py
+++ b/solution.py
@@ -257,16 +257,16 @@
     edge = SHIFT * cols
 
     def pool():
-        pixel_rows = rows_ref[...]
-        for phase in sorted({v * cols * pixels % LANES for v in range(var_count)}):
-            if phase:
-                pixel_rows = jnp.where(
-                    lax.rem(me * (cols * pixels), LANES) == phase,
-                    pltpu.roll(rows_ref[...], width - phase, 1),
-                    pixel_rows,
-                )
         for j in range(cols):
-            piece = pixel_rows[:, j * pixels : j * pixels + LANES]
+            first = lax.rem(me * (cols * pixels), LANES) + j * pixels
+            tile = first // LANES
+            shift = LANES - lax.rem(first, LANES)
+            after = jnp.minimum(tile + 1, width // LANES - 1)
+            low_part, high_part = (
+                pltpu.roll(rows_ref[:, pl.ds(pl.multiple_of(at * LANES, LANES), LANES)], lax.rem(shift, LANES), 1)
+                for at in (tile, after)
+            )
+            piece = jnp.where(lane_id < shift, low_part, high_part)
             token_ref[pl.ds(j, levels * rows, stride=cols), :] = jnp.where(
                 lane_id < pixels, piece, marks
             )

time: 13.4 us -> 13.3 us (level)
  no operation moved by 1% of the time
where the time goes in v5:
time: 13.3 us; the launch traced here: 13.1 us
  Pallas kernels  13.1 us (98%)
    pallas_call x1, Pallas kernels, body(): pl.pallas_call(functools.partial(launch, sizes), out_shape=jax.ShapeDtype...  12.4 us
    pallas_call x1, Pallas kernels, body(): pl.pallas_call(functools.partial(finish, (latents, cols, SHIFT * cols, co...  0.71 us

profile of v5, /device:TPU:0, one launch (start us, length us, event | category | flops | bytes accessed | tf_op | source)
XLA Modules:
  0.0 13.1 jit_solution(7168408889434905748)
XLA Ops:
  0.0 12.4 %shard_map.136.res_ref = f32[224,512]{1,0:T(8,128)S(1)} custom-call(bf16[1,6,3840]{2,1,0:T(8,128)(2,1)} %refs_0_.1, bf16[4,512]{1,0:T(4,128)(2,1)} %refs_1_.1, bf16[80,512]{1,0:T(8,128)(2,1)} %refs_2_.1, bf16[3,512]{1,0:T(4,128)(2,1)} %refs_3_.1, bf16[512,512]{1,0:T(8,128)(2,1)} %refs_4_.1, bf16[512,512]{1,0:T(8,128)(2,1)} %refs_5_.1, ...), custom_call_target="tpu_custom_call" | custom-call | tf_op jit(solution)/shard_map/pallas_call | solution.py:490
  12.4 0.7 %shard_map.137 = bf16[3,6,12,512]{3,2,1,0:T(8,128)(2,1)} custom-call(f32[224,512]{1,0:T(8,128)S(1)} %shard_map.136.res_ref), custom_call_target="tpu_custom_call" | custom-call | tf_op jit(solution)/shard_map/pallas_call | solution.py:516

commit v6 on v5

--- a/solution.py
+++ b/solution.py
@@ -271,11 +271,12 @@
                 lane_id < pixels, piece, marks
             )
         tokens = token_ref[...].astype(bf16)
-        made = dot(jnp.concatenate([tokens, tokens], axis=1), straight_ref[...])
-        value_ref[:block] = made[:block, :channels]
+        twice = jnp.concatenate([tokens, tokens], axis=1)
+        scores = dot(twice, straight_ref[:, channels:])
+        made = dot(twice, straight_ref[:, :channels])
+        value_ref[:block] = made[:block]
         for at in range(block, levels * block, block):
-            value_ref[at : at + block] = made[at : at + block, :channels] - made[:block, :channels]
-        scores = made[:, channels:]
+            value_ref[at : at + block] = made[at : at + block] - made[:block]
         pieces = [scores[l * block : (l + 1) * block] for l in range(levels)]
         highest = functools.reduce(jnp.maximum, pieces)
         weights = [jnp.exp2(piece - highest) for piece in pieces]
@@ -286,10 +287,10 @@
         shares = jnp.concatenate([high, low], axis=1)
         found = []
         for q in range(latents):
-            parts = dot(shares, widen_ref[q]) * value_ref[block:]
-            total = functools.reduce(
-                jnp.add, [parts[l * block : (l + 1) * block] for l in range(levels - 1)], value_ref[:block]
-            )
+            total = value_ref[:block]
+            wide = dot(shares, widen_ref[q])
+            for l in range(levels - 1):
+                total = total + wide[l * block : (l + 1) * block] * value_ref[(l + 1) * block : (l + 2) * block]
             found.append(total)
         joined = dot(jnp.concatenate(found, axis=0).astype(bf16), co_v[...])
         return [

time: 13.3 us -> 13.2 us (level)
  no operation moved by 1% of the time
where the time goes in v6:
time: 13.2 us; the launch traced here: 13.1 us
  Pallas kernels  13.1 us (99%)
    pallas_call x1, Pallas kernels, body(): pl.pallas_call(functools.partial(launch, sizes), out_shape=jax.ShapeDtype...  12.4 us
    pallas_call x1, Pallas kernels, body(): pl.pallas_call(functools.partial(finish, (latents, cols, SHIFT * cols, co...  0.71 us

profile of v6, /device:TPU:0, one launch (start us, length us, event | category | flops | bytes accessed | tf_op | source)
XLA Modules:
  0.0 13.1 jit_solution(1986964669336915898)
XLA Ops:
  0.0 12.4 %shard_map.136.res_ref = f32[224,512]{1,0:T(8,128)S(1)} custom-call(bf16[1,6,3840]{2,1,0:T(8,128)(2,1)} %refs_0_.1, bf16[4,512]{1,0:T(4,128)(2,1)} %refs_1_.1, bf16[80,512]{1,0:T(8,128)(2,1)} %refs_2_.1, bf16[3,512]{1,0:T(4,128)(2,1)} %refs_3_.1, bf16[512,512]{1,0:T(8,128)(2,1)} %refs_4_.1, bf16[512,512]{1,0:T(8,128)(2,1)} %refs_5_.1, ...), custom_call_target="tpu_custom_call" | custom-call | tf_op jit(solution)/shard_map/pallas_call | solution.py:491
  12.4 0.7 %shard_map.137 = bf16[3,6,12,512]{3,2,1,0:T(8,128)(2,1)} custom-call(f32[224,512]{1,0:T(8,128)S(1)} %shard_map.136.res_ref), custom_call_target="tpu_custom_call" | custom-call | tf_op jit(solution)/shard_map/pallas_call | solution.py:517

commit v7 on v6

--- a/solution.py
+++ b/solution.py
@@ -212,8 +212,8 @@
         for l in range(levels):
             inside = jnp.logical_and(row_id >= l * rows, row_id < (l + 1) * rows)
             marks = jnp.where(jnp.logical_and(inside, lane_id == pixels + l), 1.0, marks)
-        slot = lax.rem(lax.broadcasted_iota(jnp.int32, (2 * LANES, channels), 0), LANES)
-        lane = lax.broadcasted_iota(jnp.int32, (2 * LANES, channels), 1) // head
+        slot = lax.rem(lax.broadcasted_iota(jnp.int32, (LANES, channels), 0), LANES)
+        lane = lax.broadcasted_iota(jnp.int32, (LANES, channels), 1) // head
         for q in range(latents):
             widen_ref[q] = jnp.where(slot == lane + q * HEADS, 1.0, 0.0).astype(bf16)
 
@@ -282,9 +282,7 @@
         weights = [jnp.exp2(piece - highest) for piece in pieces]
         inverse = 1.0 / functools.reduce(jnp.add, weights)
         share = jnp.concatenate([weight * inverse for weight in weights[1:]], axis=0)
-        high = share.astype(bf16)
-        low = (share - high.astype(f32)).astype(bf16)
-        shares = jnp.concatenate([high, low], axis=1)
+        shares = share.astype(bf16)
         found = []
         for q in range(latents):
             total = value_ref[:block]
@@ -294,7 +292,7 @@
             found.append(total)
         joined = dot(jnp.concatenate(found, axis=0).astype(bf16), co_v[...])
         return [
-            (joined[q * block : (q + 1) * block] + queries[q : q + 1]).astype(bf16).astype(f32)
+            joined[q * block : (q + 1) * block] + queries[q : q + 1]
             for q in range(latents)
         ]
 
@@ -499,7 +497,7 @@
                 pltpu.VMEM((levels * rows, width), f32),
                 *weights,
                 pltpu.VMEM((2 * LANES, channels + LANES), bf16),
-                pltpu.VMEM((latents, 2 * LANES, channels), bf16),
+                pltpu.VMEM((latents, LANES, channels), bf16),
                 pltpu.VMEM((levels * rows * cols, LANES), f32),
                 pltpu.VMEM((levels * rows * cols, channels), f32),
                 pltpu.VMEM((4 * LANES, channels), f32),

time: 13.2 us -> 13.2 us (level)
  no operation moved by 1% of the time
where the time goes in v7:
time: 13.2 us; the launch traced here: 13.1 us
  Pallas kernels  13 us (98%)
    pallas_call x1, Pallas kernels, body(): pl.pallas_call(functools.partial(launch, sizes), out_shape=jax.ShapeDtype...  12.3 us
    pallas_call x1, Pallas kernels, body(): pl.pallas_call(functools.partial(finish, (latents, cols, SHIFT * cols, co...  0.71 us

profile of v7, /device:TPU:0, one launch (start us, length us, event | category | flops | bytes accessed | tf_op | source)
XLA Modules:
  0.0 13.1 jit_solution(13771029449690082176)
XLA Ops:
  0.0 12.3 %shard_map.136.res_ref = f32[224,512]{1,0:T(8,128)S(1)} custom-call(bf16[1,6,3840]{2,1,0:T(8,128)(2,1)} %refs_0_.1, bf16[4,512]{1,0:T(4,128)(2,1)} %refs_1_.1, bf16[80,512]{1,0:T(8,128)(2,1)} %refs_2_.1, bf16[3,512]{1,0:T(4,128)(2,1)} %refs_3_.1, bf16[512,512]{1,0:T(8,128)(2,1)} %refs_4_.1, bf16[512,512]{1,0:T(8,128)(2,1)} %refs_5_.1, ...), custom_call_target="tpu_custom_call" | custom-call | tf_op jit(solution)/shard_map/pallas_call | solution.py:489
  12.3 0.7 %shard_map.137 = bf16[3,6,12,512]{3,2,1,0:T(8,128)(2,1)} custom-call(f32[224,512]{1,0:T(8,128)S(1)} %shard_map.136.res_ref), custom_call_target="tpu_custom_call" | custom-call | tf_op jit(solution)/shard_map/pallas_call | solution.py:515

commit v8 on v6

--- a/solution.py
+++ b/solution.py
@@ -95,8 +95,6 @@
             bit *= 2
         return turned
 
-    announce()
-
     pairs = (
         (query_hbm, query_v), (ck_hbm, ck_v), (embed_hbm, embed_v), (bias_hbm, bias_v),
         (cv_hbm, cv_v), (co_hbm, co_v), (gain1_hbm, gain1_v), (wc_hbm, wc_v), (wq_hbm, wq_v),
@@ -118,6 +116,8 @@
             load_sem.at[len(pairs) + d],
         )
         stages[d].start()
+
+    announce()
 
     with jax.named_scope("F_barrier"):
         pl.semaphore_wait(
@@ -310,8 +310,8 @@
     with jax.named_scope("L_ownpool"):
         own_latent = jnp.concatenate(pool(), axis=0)
         own_normed = layer_norm(own_latent, gain1_v[...]).astype(bf16)
+        asked = dot(own_normed, wq_v[...]) * (head ** (-0.5) * math.log2(math.e))
         context = dot(own_normed, wc_v[...])
-        asked = dot(own_normed, wq_v[...]) * (head ** (-0.5) * math.log2(math.e))
     part = half
     for q in range(latents):
         for w in range(2):

time: 13.2 us -> 13.2 us (level)
  no operation moved by 1% of the time
where the time goes in v8:
time: 13.2 us; the launch traced here: 13.1 us
  Pallas kernels  13.1 us (99%)
    pallas_call x1, Pallas kernels, body(): pl.pallas_call(functools.partial(launch, sizes), out_shape=jax.ShapeDtype...  12.4 us
    pallas_call x1, Pallas kernels, body(): pl.pallas_call(functools.partial(finish, (latents, cols, SHIFT * cols, co...  0.71 us

profile of v8, /device:TPU:0, one launch (start us, length us, event | category | flops | bytes accessed | tf_op | source)
XLA Modules:
  0.0 13.1 jit_solution(9000128257770265913)
XLA Ops:
  0.0 12.4 %shard_map.136.res_ref = f32[224,512]{1,0:T(8,128)S(1)} custom-call(bf16[1,6,3840]{2,1,0:T(8,128)(2,1)} %refs_0_.1, bf16[4,512]{1,0:T(4,128)(2,1)} %refs_1_.1, bf16[80,512]{1,0:T(8,128)(2,1)} %refs_2_.1, bf16[3,512]{1,0:T(4,128)(2,1)} %refs_3_.1, bf16[512,512]{1,0:T(8,128)(2,1)} %refs_4_.1, bf16[512,512]{1,0:T(8,128)(2,1)} %refs_5_.1, ...), custom_call_target="tpu_custom_call" | custom-call | tf_op jit(solution)/shard_map/pallas_call | solution.py:491
  12.4 0.7 %shard_map.137 = bf16[3,6,12,512]{3,2,1,0:T(8,128)(2,1)} custom-call(f32[224,512]{1,0:T(8,128)S(1)} %shard_map.136.res_ref), custom_call_target="tpu_custom_call" | custom-call | tf_op jit(solution)/shard_map/pallas_call | solution.py:517

commit v9 on v6

--- a/solution.py
+++ b/solution.py
@@ -400,11 +400,11 @@
 
         turns = [(w, g, p) for w in range(2) for g in range(channels // LANES) for p in range(0, group, 2)]
         scored = {}
-        for i in range(len(turns) + 16):
+        for i in range(len(turns) + 8):
             if i < len(turns):
                 scored[i] = power_of(score(*turns[i]))
-            if i >= 16:
-                take(*turns[i - 16], scored.pop(i - 16))
+            if i >= 8:
+                take(*turns[i - 8], scored.pop(i - 8))
 
     with jax.named_scope("R_wo"):
         mixes = [mix_ref[:, w * LANES : (w + 1) * LANES].T[:count] for w in range(2)]

time: 13.2 us -> 13.2 us (level)
  no operation moved by 1% of the time
where the time goes in v9:
time: 13.2 us; the launch traced here: 13 us
  Pallas kernels  13 us (98%)
    pallas_call x1, Pallas kernels, body(): pl.pallas_call(functools.partial(launch, sizes), out_shape=jax.ShapeDtype...  12.3 us
    pallas_call x1, Pallas kernels, body(): pl.pallas_call(functools.partial(finish, (latents, cols, SHIFT * cols, co...  0.71 us

profile of v9, /device:TPU:0, one launch (start us, length us, event | category | flops | bytes accessed | tf_op | source)
XLA Modules:
  0.0 13.0 jit_solution(11516632614425921992)
XLA Ops:
  0.0 12.3 %shard_map.136.res_ref = f32[224,512]{1,0:T(8,128)S(1)} custom-call(bf16[1,6,3840]{2,1,0:T(8,128)(2,1)} %refs_0_.1, bf16[4,512]{1,0:T(4,128)(2,1)} %refs_1_.1, bf16[80,512]{1,0:T(8,128)(2,1)} %refs_2_.1, bf16[3,512]{1,0:T(4,128)(2,1)} %refs_3_.1, bf16[512,512]{1,0:T(8,128)(2,1)} %refs_4_.1, bf16[512,512]{1,0:T(8,128)(2,1)} %refs_5_.1, ...), custom_call_target="tpu_custom_call" | custom-call | tf_op jit(solution)/shard_map/pallas_call | solution.py:491
  12.3 0.7 %shard_map.137 = bf16[3,6,12,512]{3,2,1,0:T(8,128)(2,1)} custom-call(f32[224,512]{1,0:T(8,128)S(1)} %shard_map.136.res_ref), custom_call_target="tpu_custom_call" | custom-call | tf_op jit(solution)/shard_map/pallas_call | solution.py:517
